TPU v7x, 32 devices: a whole 2x2x4 slice. The times are simulated.
32 devices in a mesh: leaf: 8 (over z, x), row: 2 (over y), col: 2 (over core).
Axes of the slice: x: 2, y: 2, z: 4, core: 2. Of those that a mesh axis runs over, the one named last changes fastest.
Arguments:
- leaf_rhs: bfloat16 [8, 4096, 128], P('leaf', ('row', 'col')), may hold values from -6 to 6
- leaf_factor: bfloat16 [8, 4096, 4096], P('leaf', ('row', 'col')), as said below
- leaf_coupling: bfloat16 [8, 4096, 4096], P('leaf', None, ('row', 'col')), may hold values from -0.046875 to 0.046875
- border_rows: int32 [8, 4096], P('leaf'), may hold values from 0 to 4095, as said below
- border_count: int32 [8], P('leaf'), may hold values from 1024 to 4096, as said below
- separator_rhs: bfloat16 [4096, 128], P(('leaf', 'row', 'col')), may hold values from -6 to 6
- separator_factor: bfloat16 [4096, 4096], P(('leaf', 'row', 'col')), as said below
Outputs:
- leaf_solution: float32 [8, 4096, 128], P('leaf', ('row', 'col'))
- separator_solution: float32 [4096, 128], P(('leaf', 'row', 'col'))
Inputs may be any that keep to these rules, and one draw needn't show every extreme that they name: `border_rows`: the 4096 row numbers of one section are distinct. Border rows j < border_count[k] of section k are live, the others are unused; some section has all 4096 live. `leaf_factor`: lower triangular with a positive diagonal. `separator_factor`: lower triangular with a positive diagonal.
All inputs are finite; a program needn't handle non-finite values.
Results may differ from a plain program's by a relative error of at most 0.013.
Values may be sent and summed in bfloat16 or wider, within the bound.
No kernel may reach another device: no remote copies, remote signals or barrier semaphores. Data moves between devices by JAX's collectives and lax.ppermute only.
A program may use at most 64 MiB of HBM per device.

v0:
```python
import jax
import jax.numpy as jnp
from jax import lax
from jax.sharding import PartitionSpec as P


def local(
    leaf_rhs, leaf_factor, leaf_coupling, border_rows, border_count, separator_rhs, separator_factor
):
    contract_first = (((0,), (0,)), ((), ()))
    rhs_local = leaf_rhs[0]
    factor_local = leaf_factor[0]
    coupling = leaf_coupling[0]
    index_set = border_rows[0]
    live = jnp.arange(index_set.shape[0], dtype=jnp.int32) < border_count[0]
    columns = rhs_local.shape[1]
    block = factor_local
    forward = jnp.dot(
        block,
        lax.all_gather(rhs_local, ("row", "col"), axis=0, tiled=True),
        preferred_element_type=jnp.float32,
    ).astype(jnp.bfloat16)
    update = jnp.dot(coupling, forward, preferred_element_type=jnp.float32)
    update = jnp.where(live[:, None], update, 0.0)
    sep_rows = separator_factor.shape[0]
    sep_order = separator_factor.shape[1]
    position = lax.axis_index(("leaf", "row", "col")) * sep_rows
    placed = lax.dynamic_update_slice_in_dim(
        jnp.zeros((sep_order, columns), jnp.float32), separator_rhs.astype(jnp.float32), position, 0
    )
    placed = placed.at[index_set].add(-update)
    whole = lax.psum(placed, ("leaf", "row", "col")).astype(jnp.bfloat16)
    root_forward = jnp.dot(separator_factor, whole, preferred_element_type=jnp.float32).astype(
        jnp.bfloat16
    )
    partial_terms = lax.dot_general(
        separator_factor, root_forward, contract_first, preferred_element_type=jnp.float32
    )
    totals = lax.psum(partial_terms, ("leaf", "row", "col"))
    separator_solution = lax.dynamic_slice_in_dim(totals, position, sep_rows, 0)
    rounded = totals.astype(jnp.bfloat16)
    border = jnp.where(live[:, None], rounded[index_set], jnp.zeros((), jnp.bfloat16))
    corrected = (
        forward.astype(jnp.float32)
        - lax.dot_general(coupling, border, contract_first, preferred_element_type=jnp.float32)
    ).astype(jnp.bfloat16)
    block = factor_local
    solution = lax.psum_scatter(
        lax.dot_general(
            block, corrected, contract_first, preferred_element_type=jnp.float32
        ).astype(jnp.bfloat16),
        ("row", "col"),
        scatter_dimension=0,
        tiled=True,
    ).astype(jnp.float32)
    return (solution[None], separator_solution)


def solution(mesh):
    placed = (
        P("leaf", ("row", "col"), None),
        P("leaf", ("row", "col"), None),
        P("leaf", None, ("row", "col")),
        P("leaf", None),
        P("leaf"),
        P(("leaf", "row", "col"), None),
        P(("leaf", "row", "col"), None),
    )
    return jax.shard_map(
        local,
        mesh=mesh,
        in_specs=placed,
        out_specs=(P("leaf", ("row", "col"), None), P(("leaf", "row", "col"), None)),
        check_vma=False,
    )
```

profile of v0, /device:TPU:0, one launch (start us, length us, event | category | flops | bytes accessed | tf_op | source)
XLA Modules:
  0.0 322.0 jit_solution(7589405319605890312)
XLA Ops:
  7.2 0.0 copy-start
  7.2 0.0 copy-start.2
  7.2 0.0 copy-start.3
  7.2 0.0 all-gather.3.cloned.1.call-start
  7.2 0.7 all-gather.3.cloned.1.call-update
  7.9 0.0 all-reduce.3.cloned.1.call-start
  8.6 0.1 broadcast_in_dim.38
  8.8 0.0 copy-done.2
  8.8 0.0 copy-done.3
  8.9 20.2 %all-gather.3.cloned.1.call-done = bf16[1,4096,128]{2,1,0:T(8,128)(2,1)} async-done(((bf16[1,1024,128]{2,1,0:T(8,128)(2,1)}), bf16[1,4096,128]{2,1,0:T(8,128)(2,1)}) %all-gather.3.cloned.1.call-update) | async-done | bytes 1048592 | tf_op jit(solution)/shard_map/all_gather | solution.py:20
  29.0 0.0 copy-start.1
  29.0 6.1 %fusion.32 = bf16[1024,128]{1,0:T(8,128)(2,1)S(1)} fusion(bf16[1,1024,4096]{2,1,0:T(8,128)(2,1)} %param.8, bf16[1,4096,128]{2,1,0:T(8,128)(2,1)} %all-gather.3.cloned.1.call-done), kind=kOutput, calls=%fused_computation.19 | convolution fusion | flops 1073872896 | bytes 9699328 | tf_op jit(solution)/shard_map/dot_general | solution.py:18
  35.1 0.0 copy-done.1
  35.1 4.4 %fusion.17 = f32[4096,128]{1,0:T(8,128)} fusion(bf16[1024,128]{1,0:T(8,128)(2,1)S(1)} %fusion.32, bf16[1,4096,1024]{2,1,0:T(8,128)(2,1)S(1)} %copy-done.1, pred[4096]{0:T(1024)(128)(4,1)S(1)} %iota_compare_fusion), kind=kOutput, calls=%fused_computation.14 | convolution fusion | flops 1074790400 | bytes 10752000 | tf_op jit(solution)/shard_map/dot_general | solution.py:23
  39.5 23.4 %scatter_fusion = f32[4096,128]{1,0:T(8,128)S(1)} fusion(f32[4096,128]{1,0:T(8,128)S(1)} %convert_dynamic-update-slice_fusion, s32[4096]{0:T(1024)S(1)} %bitcast.59, f32[4096,128]{1,0:T(8,128)} %fusion.17), kind=kCustom, calls=%fused_computation.1 | custom fusion | flops 524288 | bytes 6307840 | tf_op jit(solution)/shard_map/scatter-add | solution.py:31
  63.0 62.4 %all-reduce.4 = bf16[4096,128]{1,0:T(8,128)(2,1)} all-reduce(f32[4096,128]{1,0:T(8,128)S(1)} %scatter_fusion), channel_id=1, replica_groups=mesh['leaf'=8,'row'=2,'col'=2] {'leaf','row','col'}, use_global_device_ids=true, to_apply=%region_1.2 | all-reduce | flops 524288 | bytes 3145728 | tf_op jit(solution)/shard_map/psum | solution.py:32
  125.3 0.0 copy-done
  125.3 3.9 %convolution_bitcast_fusion = f32[4096,128]{0,1:T(8,128)} fusion(bf16[128,4096]{1,0:T(8,128)(2,1)S(1)} %copy-done, bf16[4096,128]{1,0:T(8,128)(2,1)} %all-reduce.4), kind=kOutput, calls=%fused_computation.10 | convolution fusion | flops 268451840 | bytes 4194304 | tf_op jit(solution)/shard_map/dot_general | solution.py:36
  129.2 0.0 all-reduce.3.cloned.1.call-update
  129.2 0.2 reduce-scatter.2.cloned.1.call-start
  129.5 133.4 %all-reduce.3.cloned.1.call-done = f32[4096,128]{0,1:T(8,128)} async-done(((f32[4096,128]{0,1:T(8,128)}), f32[4096,128]{0,1:T(8,128)}) %all-reduce.3.cloned.1.call-update) | async-done | bytes 2097168 | tf_op jit(solution)/shard_map/psum | solution.py:39
  262.8 1.7 convert_element_type.34
  264.6 0.7 copy.12
  265.2 12.1 %gather_fusion = bf16[4096,128]{1,0:T(8,128)(2,1)S(1)} fusion(bf16[4096,128]{1,0:T(8,128)(2,1)S(1)} %copy.12, s32[4096]{0:T(1024)S(1)} %broadcast_clamp_fusion), kind=kCustom, calls=%fused_computation | custom fusion | bytes 2113536 | tf_op jit(solution)/shard_map/gather | solution.py:42
  277.4 12.4 %fusion.20 = bf16[4096,128]{0,1:T(8,128)(2,1)} fusion(bf16[1,1024,4096]{2,1,0:T(8,128)(2,1)} %param.8, bf16[1,4096,1024]{2,1,0:T(8,128)(2,1)} %param.9, bf16[4096,128]{1,0:T(8,128)(2,1)S(1)} %gather_fusion, pred[4096]{0:T(1024)(128)(4,1)S(1)} %iota_compare_fusion, bf16[1024,128]{1,0:T(8,128)(2,1)S(1)} %fusion.32), kind=kOutput, calls=%fused_computation.15 | convolution fusion | flops 2148925440 | bytes 19140608 | tf_op jit(solution)/shard_map/dot_general | solution.py:49
  289.8 0.0 reduce-scatter.2.cloned.1.call-update
  289.8 0.9 constant_dynamic-slice_fusion
  290.6 0.7 copy.14
  291.4 22.1 %reduce-scatter.2.cloned.1.call-done = bf16[1024,128]{0,1:T(8,128)(2,1)} async-done(((bf16[4096,128]{0,1:T(8,128)(2,1)}), bf16[1024,128]{0,1:T(8,128)(2,1)}) %reduce-scatter.2.cloned.1.call-update) | async-done | bytes 262160 | tf_op jit(solution)/shard_map/reduce_scatter | solution.py:48
  313.5 1.0 bitcast_convert_fusion
  314.5 1.0 copy.13
  (4 shorter events, 0.0 us)
Async XLA Ops:
  7.2 118.2 %copy-start = (bf16[128,4096]{1,0:T(8,128)(2,1)S(1)}, bf16[128,4096]{1,0:T(8,128)(2,1)}, u32[]{:S(2)}) copy-start(bf16[128,4096]{1,0:T(8,128)(2,1)} %param.13) | copy-start | bytes 3145732
  7.2 1.6 copy-start.2
  7.2 1.6 copy-start.3
  7.2 21.8 %all-gather.3.cloned.1.call-start = ((), (), s32[]{:S(2)}) async-start(), calls=%async_computation.3 | async-start | bytes 1310720 | tf_op jit(solution)/shard_map/all_gather | solution.py:20
  7.9 254.9 %all-reduce.3.cloned.1.call-start = ((), (), s32[]{:S(2)}) async-start(), calls=%async_computation.1 | async-start | bytes 4194304 | tf_op jit(solution)/shard_map/psum | solution.py:39
  29.0 6.1 %copy-start.1 = (bf16[1,4096,1024]{2,1,0:T(8,128)(2,1)S(1)}, bf16[1,4096,1024]{2,1,0:T(8,128)(2,1)}, u32[]{:S(2)}) copy-start(bf16[1,4096,1024]{2,1,0:T(8,128)(2,1)} %param.9) | copy-start | bytes 25165828
  129.2 184.3 %reduce-scatter.2.cloned.1.call-start = ((), (), s32[]{:S(2)}) async-start(), calls=%async_computation.2 | async-start | bytes 1310720 | tf_op jit(solution)/shard_map/reduce_scatter | solution.py:48
Sparse Core Ops, SparseCore 0:
  9.6 19.4 all-gather.2
  129.4 133.4 all-reduce.2
  289.9 23.5 reduce-scatter.1
where the time goes:
time: 322 us
  waiting for transfers between devices  176 us (55%)
  blocking collectives  62.4 us (19%)
  matrix products  26.7 us (8%)
  other arithmetic  26.2 us (8%)
  local copies, waits for them, and re-layouts  15.5 us (5%)
  between operations  14.5 us (5%)
    psum x1, waiting for transfers between devices, local(): totals = lax.psum(partial_terms, ('leaf', 'row', 'col'))  133 us
    psum x1, blocking collectives, local(): whole = lax.psum(placed, ('leaf', 'row', 'col')).astype(jnp.bfloat16)  62.4 us
    scatter-add x1, other arithmetic, local(): placed = placed.at[index_set].add(-update)  23.4 us
    reduce_scatter x1, waiting for transfers between devices, local(): lax.psum_scatter(lax.dot_general(block, corrected, contract_first, prefer...  22.1 us
    all_gather x1, waiting for transfers between devices, local(): lax.all_gather(rhs_local, ('row', 'col'), axis=0, tiled=True)  20.2 us
    dot_general x1, matrix products, local(): lax.dot_general(block, corrected, contract_first, preferred_element_type=...  12.4 us
    gather x1, local copies, waits for them, and re-layouts, local(): rounded[index_set]  12.1 us
  transfers between devices with their start and end apart: 3, of which 3 were waited for; matrix products, arithmetic and copies ran while one was open for 1% of the time, Pallas kernels for 0%

commit v1 on v0

--- a/solution.py
+++ b/solution.py
@@ -2,6 +2,10 @@
 import jax.numpy as jnp
 from jax import lax
 from jax.sharding import PartitionSpec as P
+
+report_spans_on = lambda x_in, ax_name, shard_axis: lax.psum(
+    lax.psum(x_in, axis_name=ax_name), shard_axis
+)
 
 
 def local(
@@ -29,7 +33,7 @@
         jnp.zeros((sep_order, columns), jnp.float32), separator_rhs.astype(jnp.float32), position, 0
     )
     placed = placed.at[index_set].add(-update)
-    whole = lax.psum(placed, ("leaf", "row", "col")).astype(jnp.bfloat16)
+    whole = report_spans_on(placed, "leaf", ("row", "col")).astype(jnp.bfloat16)
     root_forward = jnp.dot(separator_factor, whole, preferred_element_type=jnp.float32).astype(
         jnp.bfloat16
     )

time: 322 us -> 404 us (1.25)
  waiting for transfers between devices: 176 us -> 280 us
  blocking collectives: 62.4 us -> 41 us
    psum x0 -> x1, waiting for transfers between devices: none -> 102 us  [lax.psum(x_in, axis_name=ax_name)]
    psum x1, blocking collectives: 62.4 us -> 41 us  [lax.psum(lax.psum(x_in, axis_name=ax_name), shard_axis)]
  transfers between devices with their start and end apart: 3 -> 4, of which waited for: 3 -> 4; matrix products, arithmetic and copies ran while one was open for 1% -> 0% of each run, Pallas kernels for 0% -> 0%
where the time goes in v1:
time: 404 us
  waiting for transfers between devices  280 us (69%)
  blocking collectives  41 us (10%)
  other arithmetic  26.2 us (6%)
  matrix products  25.5 us (6%)
  local copies, waits for them, and re-layouts  16.8 us (4%)
  between operations  14.6 us (4%)
    psum x1, waiting for transfers between devices, local(): totals = lax.psum(partial_terms, ('leaf', 'row', 'col'))  134 us
    psum x1, waiting for transfers between devices, lax.psum(x_in, axis_name=ax_name)  102 us
    psum x1, blocking collectives, lax.psum(lax.psum(x_in, axis_name=ax_name), shard_axis)  41 us
    scatter-add x1, other arithmetic, local(): placed = placed.at[index_set].add(-update)  23.4 us
    reduce_scatter x1, waiting for transfers between devices, local(): lax.psum_scatter(lax.dot_general(block, corrected, contract_first, prefer...  22.1 us
    all_gather x1, waiting for transfers between devices, local(): lax.all_gather(rhs_local, ('row', 'col'), axis=0, tiled=True)  20.2 us
    dot_general x1, matrix products, local(): lax.dot_general(block, corrected, contract_first, preferred_element_type=...  12.4 us
    gather x1, local copies, waits for them, and re-layouts, local(): rounded[index_set]  12.1 us
  transfers between devices with their start and end apart: 4, of which 4 were waited for; matrix products, arithmetic and copies ran while one was open for 0% of the time, Pallas kernels for 0%

profile of v1, /device:TPU:0, one launch (start us, length us, event | category | flops | bytes accessed | tf_op | source)
XLA Modules:
  0.0 404.0 jit_solution(13632580934254791846)
XLA Ops:
  7.2 0.0 copy-start
  7.2 0.0 copy-start.3
  7.2 0.0 copy-start.4
  7.2 0.0 all-gather.3.cloned.1.call-start
  7.2 0.7 all-gather.3.cloned.1.call-update
  7.9 0.0 all-reduce.4.cloned.1.call-start
  8.6 0.1 broadcast_in_dim.38
  8.8 0.0 copy-done.4
  8.9 20.2 %all-gather.3.cloned.1.call-done = bf16[1,4096,128]{2,1,0:T(8,128)(2,1)} async-done(((bf16[1,1024,128]{2,1,0:T(8,128)(2,1)}), bf16[1,4096,128]{2,1,0:T(8,128)(2,1)}) %all-gather.3.cloned.1.call-update) | async-done | bytes 1048592 | tf_op jit(solution)/shard_map/all_gather | solution.py:24
  29.0 6.1 %fusion.32 = bf16[1024,128]{1,0:T(8,128)(2,1)S(1)} fusion(bf16[1,1024,4096]{2,1,0:T(8,128)(2,1)} %param.8, bf16[1,4096,128]{2,1,0:T(8,128)(2,1)} %all-gather.3.cloned.1.call-done), kind=kOutput, calls=%fused_computation.19 | convolution fusion | flops 1073872896 | bytes 9699328 | tf_op jit(solution)/shard_map/dot_general | solution.py:22
  35.1 0.0 copy-done.2
  35.1 4.4 %fusion.17 = f32[4096,128]{1,0:T(8,128)} fusion(bf16[1024,128]{1,0:T(8,128)(2,1)S(1)} %fusion.32, bf16[1,4096,1024]{2,1,0:T(8,128)(2,1)S(1)} %copy-done.2, pred[4096]{0:T(1024)(128)(4,1)S(1)} %iota_compare_fusion), kind=kOutput, calls=%fused_computation.14 | convolution fusion | flops 1074790400 | bytes 10752000 | tf_op jit(solution)/shard_map/dot_general | solution.py:27
  39.5 23.4 %scatter_fusion = f32[4096,128]{1,0:T(8,128)S(1)} fusion(f32[4096,128]{1,0:T(8,128)S(1)} %convert_dynamic-update-slice_fusion, s32[4096]{0:T(1024)S(1)} %bitcast.59, f32[4096,128]{1,0:T(8,128)} %fusion.17), kind=kCustom, calls=%fused_computation.1 | custom fusion | flops 524288 | bytes 6307840 | tf_op jit(solution)/shard_map/scatter-add | solution.py:35
  63.0 1.3 copy-done.1
  64.3 0.0 all-reduce.4.cloned.1.call-update
  64.3 0.0 all-reduce.6.cloned.1.call-start
  64.4 102.4 %all-reduce.4.cloned.1.call-done = f32[4096,128]{1,0:T(8,128)} async-done(((f32[4096,128]{1,0:T(8,128)}), f32[4096,128]{1,0:T(8,128)}) %all-reduce.4.cloned.1.call-update) | async-done | bytes 2097168 | tf_op jit(solution)/shard_map/psum | solution.py:7
  166.8 41.0 %all-reduce.7 = bf16[4096,128]{1,0:T(8,128)(2,1)S(1)} all-reduce(f32[4096,128]{1,0:T(8,128)} %all-reduce.4.cloned.1.call-done), channel_id=1, replica_groups=mesh['leaf'=8,'row'=2,'col'=2] {'row','col'}, use_global_device_ids=true, to_apply=%region_2.3 | all-reduce | flops 524288 | bytes 3145728 | tf_op jit(solution)/shard_map/psum | solution.py:6
  207.8 2.6 convolution_bitcast_fusion
  210.4 0.0 all-reduce.6.cloned.1.call-update
  210.4 0.2 reduce-scatter.2.cloned.1.call-start
  210.7 134.2 %all-reduce.6.cloned.1.call-done = f32[4096,128]{0,1:T(8,128)} async-done(((f32[4096,128]{0,1:T(8,128)}), f32[4096,128]{0,1:T(8,128)}) %all-reduce.6.cloned.1.call-update) | async-done | bytes 2097168 | tf_op jit(solution)/shard_map/psum | solution.py:43
  344.8 1.7 convert_element_type.34
  346.6 0.7 copy.12
  347.2 12.1 %gather_fusion = bf16[4096,128]{1,0:T(8,128)(2,1)S(1)} fusion(bf16[4096,128]{1,0:T(8,128)(2,1)S(1)} %copy.12, s32[4096]{0:T(1024)S(1)} %broadcast_clamp_fusion), kind=kCustom, calls=%fused_computation | custom fusion | bytes 2113536 | tf_op jit(solution)/shard_map/gather | solution.py:46
  359.4 12.4 %fusion.20 = bf16[4096,128]{0,1:T(8,128)(2,1)} fusion(bf16[1,1024,4096]{2,1,0:T(8,128)(2,1)} %param.8, bf16[1,4096,1024]{2,1,0:T(8,128)(2,1)} %param.9, bf16[4096,128]{1,0:T(8,128)(2,1)S(1)} %gather_fusion, pred[4096]{0:T(1024)(128)(4,1)S(1)} %iota_compare_fusion, bf16[1024,128]{1,0:T(8,128)(2,1)S(1)} %fusion.32), kind=kOutput, calls=%fused_computation.15 | convolution fusion | flops 2148925440 | bytes 19140608 | tf_op jit(solution)/shard_map/dot_general | solution.py:53
  371.8 0.0 reduce-scatter.2.cloned.1.call-update
  371.8 0.9 constant_dynamic-slice_fusion
  372.7 0.7 copy.14
  373.4 22.1 %reduce-scatter.2.cloned.1.call-done = bf16[1024,128]{0,1:T(8,128)(2,1)} async-done(((bf16[4096,128]{0,1:T(8,128)(2,1)}), bf16[1024,128]{0,1:T(8,128)(2,1)}) %reduce-scatter.2.cloned.1.call-update) | async-done | bytes 262160 | tf_op jit(solution)/shard_map/reduce_scatter | solution.py:52
  395.5 1.0 bitcast_convert_fusion
  396.5 1.0 copy.13
  (8 shorter events, 0.1 us)
Async XLA Ops:
  7.2 200.6 %copy-start = (bf16[128,4096]{1,0:T(8,128)(2,1)S(1)}, bf16[128,4096]{1,0:T(8,128)(2,1)}, u32[]{:S(2)}) copy-start(bf16[128,4096]{1,0:T(8,128)(2,1)} %param.13) | copy-start | bytes 3145732
  7.2 1.6 copy-start.3
  7.2 1.6 copy-start.4
  7.2 21.8 %all-gather.3.cloned.1.call-start = ((), (), s32[]{:S(2)}) async-start(), calls=%async_computation.4 | async-start | bytes 1310720 | tf_op jit(solution)/shard_map/all_gather | solution.py:24
  7.9 158.8 %all-reduce.4.cloned.1.call-start = ((), (), s32[]{:S(2)}) async-start(), calls=%async_computation.1 | async-start | bytes 4194304 | tf_op jit(solution)/shard_map/psum | solution.py:7
  29.0 6.1 %copy-start.2 = (bf16[1,4096,1024]{2,1,0:T(8,128)(2,1)S(1)}, bf16[1,4096,1024]{2,1,0:T(8,128)(2,1)}, u32[]{:S(2)}) copy-start(bf16[1,4096,1024]{2,1,0:T(8,128)(2,1)} %param.9) | copy-start | bytes 25165828
  63.0 1.3 copy-start.1
  64.3 280.5 %all-reduce.6.cloned.1.call-start = ((), (), s32[]{:S(2)}) async-start(), calls=%async_computation.2 | async-start | bytes 4194304 | tf_op jit(solution)/shard_map/psum | solution.py:43
  210.4 185.1 %reduce-scatter.2.cloned.1.call-start = ((), (), s32[]{:S(2)}) async-start(), calls=%async_computation.3 | async-start | bytes 1310720 | tf_op jit(solution)/shard_map/reduce_scatter | solution.py:52
Sparse Core Ops, SparseCore 0:
  9.6 19.4 all-gather.2
  64.4 102.2 all-reduce.3
  210.5 134.2 all-reduce.5
  371.9 23.5 reduce-scatter.1
